TPU v7x, 32 devices: a whole 2x2x4 slice. The times are simulated.
32 devices in a mesh: segment: 4 (over y, x), dom: 8 (over z, core).
Axes of the slice: x: 2, y: 2, z: 4, core: 2. Of those that a mesh axis runs over, the one named last changes fastest.
Arguments:
- features: bfloat16 [4, 4096, 512], P(None, 'dom'), may hold values from -6 to 6
- send_rows: int32 [4, 8, 8, 128], P(None, 'dom'), may hold values from 0 to 511
- send_len: int32 [4, 8, 8], P(None, 'dom'), may hold values from 0 to 128, as said below
- tile_src: int32 [4, 32, 4], P(None, 'dom'), may hold values from 0 to 11
- tile_count: int32 [4, 32], P(None, 'dom'), may hold values from 1 to 4, as said below
- tile_val: bfloat16 [4, 32, 4, 128, 128], P(None, 'dom'), may hold values from -0.25 to 0.25
- w_self: bfloat16 [4, 512, 512], P('segment'), may hold values from -0.25 to 0.25
- w_neigh: bfloat16 [4, 512, 512], P('segment'), may hold values from -0.25 to 0.25
- gain: bfloat16 [4, 512], P('segment'), may hold values from 0.25 to 1.75
- bias: bfloat16 [4, 512], P('segment'), may hold values from -3 to 3
Outputs:
- acts: bfloat16 [4, 4, 4096, 512], P('segment', None, 'dom')
Inputs may be any that keep to these rules, and one draw needn't show every extreme that they name: `send_len`: A partition sends nothing to itself; in every span each partition sends a full block of 128 rows to one other partition. `tile_count`: in every span one partition has 4 live tiles in each of its blocks.
All inputs are finite; a program needn't handle non-finite values.
Results may differ from a plain program's by a relative error of at most 0.0065.
Values may be sent and summed in bfloat16 or wider, within the bound.
No kernel may reach another device: no remote copies, remote signals or barrier semaphores. Data moves between devices by JAX's collectives and lax.ppermute only.
A program may use at most 64 MiB of HBM per device.

v0:
```python
import jax
import jax.numpy as jnp
from jax import lax
from jax.sharding import PartitionSpec as P

norm_eps = 1e-05


def select_span(array_in, span_id):
    return lax.dynamic_index_in_dim(array_in, span_id, 0, keepdims=False)


def sage_layer(inputs, span_id, graph, w_one, w_two, gain_one, bias_one):
    rows_all, lens_all, src_all, count_all, vals_all = graph
    send_list = select_span(rows_all, span_id)[0]
    send_count = select_span(lens_all, span_id)[0]
    tile_index = select_span(src_all, span_id)
    tile_total = select_span(count_all, span_id)
    tile_vals = select_span(vals_all, span_id)
    peer_count, tile_rows = send_list.shape
    feat_width = inputs.shape[1]
    block_count, tile_depth = tile_index.shape
    picked = jnp.take(inputs, send_list.reshape(-1), axis=0).reshape(
        peer_count, tile_rows, feat_width
    )
    row_live = lax.broadcasted_iota(jnp.int32, (peer_count, tile_rows), 1) < send_count[:, None]
    outgoing = jnp.where(row_live[:, :, None], picked, jnp.zeros_like(picked))
    incoming = lax.all_to_all(outgoing, "dom", split_axis=0, concat_axis=0, tiled=True)
    sources = jnp.concatenate(
        [inputs.reshape(block_count, tile_rows, feat_width), incoming], axis=0
    )
    tile_live = lax.broadcasted_iota(jnp.int32, (block_count, tile_depth), 1) < tile_total[:, None]

    def block_sum(packed):
        block_index, block_vals, block_live = packed
        chosen = jnp.take(sources, block_index, axis=0)
        masked = jnp.where(block_live[:, None, None], block_vals, jnp.zeros_like(block_vals))
        return jnp.einsum("kij,kjd->id", masked, chosen, preferred_element_type=jnp.float32)

    summed = lax.map(block_sum, (tile_index, tile_vals, tile_live))
    gathered = summed.reshape(block_count * tile_rows, feat_width).astype(jnp.bfloat16)
    mixed = jnp.dot(inputs, w_one, preferred_element_type=jnp.float32) + jnp.dot(
        gathered, w_two, preferred_element_type=jnp.float32
    )
    center = mixed - jnp.mean(mixed, axis=1, keepdims=True)
    spread = jnp.mean(center * center, axis=1, keepdims=True)
    scaled = center * lax.rsqrt(spread + norm_eps) * gain_one.astype(jnp.float32) + bias_one.astype(
        jnp.float32
    )
    return jnp.maximum(scaled, 0.0).astype(jnp.bfloat16)


def per_device(
    features, send_rows, send_len, tile_src, tile_count, tile_val, w_self, w_neigh, gain, bias
):
    segments = lax.axis_size("segment")
    segment_id = lax.axis_index("segment")
    span_total, node_rows, feat_width = features.shape
    graph = (send_rows, send_len, tile_src, tile_count, tile_val)
    every_self, every_neigh, every_gain, every_bias = (
        lax.all_gather(w_self, "segment", axis=0, tiled=True),
        lax.all_gather(w_neigh, "segment", axis=0, tiled=True),
        lax.all_gather(gain, "segment", axis=0, tiled=True),
        lax.all_gather(bias, "segment", axis=0, tiled=True),
    )
    span_group = span_total // segments
    layers = every_self.shape[0]
    span_id = segment_id * span_group + 0
    hidden = select_span(features, span_id)
    outputs = []
    for layer_id in range(layers):
        hidden = sage_layer(
            hidden,
            span_id,
            graph,
            every_self[layer_id],
            every_neigh[layer_id],
            every_gain[layer_id],
            every_bias[layer_id],
        )
        outputs.append(hidden)
    finished = [jnp.stack(outputs)]
    dealt_out = jnp.stack(finished, axis=1)
    return lax.all_to_all(dealt_out, "segment", split_axis=0, concat_axis=1, tiled=True)


def solution(mesh):
    in_specs = (
        P(None, "dom", None),
        P(None, "dom", None, None),
        P(None, "dom", None),
        P(None, "dom", None),
        P(None, "dom"),
        P(None, "dom", None, None, None),
        P("segment", None, None),
        P("segment", None, None),
        P("segment", None),
        P("segment", None),
    )
    out_specs = P("segment", None, "dom", None)
    return jax.shard_map(
        per_device, mesh=mesh, in_specs=in_specs, out_specs=out_specs, check_vma=False
    )
```

profile of v0, /device:TPU:0, one launch (start us, length us, event | category | flops | bytes accessed | tf_op | source)
XLA Modules:
  0.0 296.5 jit_solution(8535459585677246511)
XLA Ops:
  8.2 5.1 %gather_fusion.4 = bf16[1024,512]{1,0:T(8,128)(2,1)} fusion(bf16[512,512]{1,0:T(8,128)(2,1)S(1)} %fusion.67, s32[1024]{0:T(1024)S(1)} %fusion.49), kind=kCustom, calls=%fused_computation.clone | custom fusion | bytes 2101248 | tf_op jit(solution)/shard_map/jit(_take)/gather | solution.py:23
  14.7 1.4 broadcast_select_fusion.3
  17.3 6.5 %all-to-all-start = ((bf16[8,128,512]{2,1,0:T(8,128)(2,1)}), bf16[8,128,512]{2,1,0:T(8,128)(2,1)}, u32[]{:S(2)}, u32[]{:S(2)}) async-start(bf16[8,128,512]{2,1,0:T(8,128)(2,1)} %broadcast_select_fusion.7), calls=%async_computation | async-start | bytes 2097152 | tf_op jit(solution)/shard_map/all_to_all | solution.py:28
  24.5 8.1 %all-gather = bf16[4,1,512]{2,1,0:T(2,128)(2,1)S(1)} all-gather(bf16[1,1,512]{2,1,0:T(2,128)(2,1)S(1)} %bitcast.203), channel_id=1, replica_groups=mesh['segment'=4,'dom'=8] {'segment'}, dimensions={0}, use_global_device_ids=true | all-gather | bytes 5120 | tf_op jit(solution)/shard_map/all_gather | solution.py:63
  34.1 8.3 %all-gather.1 = bf16[4,1,512]{2,1,0:T(2,128)(2,1)S(1)} all-gather(bf16[1,1,512]{2,1,0:T(2,128)(2,1)S(1)} %bitcast.204), channel_id=1, replica_groups=mesh['segment'=4,'dom'=8] {'segment'}, dimensions={0}, use_global_device_ids=true | all-gather | bytes 5120 | tf_op jit(solution)/shard_map/all_gather | solution.py:64
  42.4 1.9 dynamic-slice_bitcast_fusion.4
  44.3 6.1 %all-to-all-done = bf16[8,128,512]{2,1,0:T(8,128)(2,1)} async-done(((bf16[8,128,512]{2,1,0:T(8,128)(2,1)}), bf16[8,128,512]{2,1,0:T(8,128)(2,1)}, u32[]{:S(2)}, u32[]{:S(2)}) %all-to-all-start) | async-done | bytes 1048608 | tf_op jit(solution)/shard_map/all_to_all | solution.py:28
  50.4 2.5 pad_maximum_fusion
  53.8 15.7 %while.40 = (s32[]{:T(128)}, bf16[4,128,512]{2,1,0:T(8,128)(2,1)}, pred[4,4]{1,0:T(4,128)(4,1)S(1)}, bf16[4,4,128,128]{3,2,1,0:T(8,128)(2,1)}, s32[4,4]{1,0:T(4,...) while((s32[]{:T(128)}, bf16[4,128,512]{2,1,0:T(8,128)(2,1)}, pred[4,4]{1,0:T(4,128)(4,1)S(1)}, ...), condition=%wide.region_1.4_spmd, body=%wide.region_0.3_spmd.sunk | while | flops 67437592 | bytes 1971369 | solution.py:40
  53.8 2.0 gather_fusion
  55.8 1.9 fusion.77
  57.8 2.0 gather_fusion
  59.8 1.9 fusion.77
  61.7 2.0 gather_fusion
  63.7 1.9 fusion.77
  65.6 2.0 gather_fusion
  67.6 1.9 fusion.77
  69.5 2.5 fusion.48
  72.0 12.2 %all-gather.7.cloned.1.call-done = bf16[4,512,512]{2,1,0:T(8,128)(2,1)} async-done(((bf16[1,512,512]{2,1,0:T(8,128)(2,1)}), bf16[4,512,512]{2,1,0:T(8,128)(2,1)}) %all-gather.7.cloned.1.call-update) | async-done | bytes 2097168 | tf_op jit(solution)/shard_map/all_gather | solution.py:62
  84.2 1.9 fusion.53
  87.4 5.1 %gather_fusion.5 = bf16[1024,512]{1,0:T(8,128)(2,1)} fusion(bf16[512,512]{1,0:T(8,128)(2,1)S(1)} %maximum_convert_fusion.3, s32[1024]{0:T(1024)S(1)} %fusion.49), kind=kCustom, calls=%fused_computation.2.clone | custom fusion | bytes 2101248 | tf_op jit(solution)/shard_map/jit(_take)/gather | solution.py:23
  92.5 1.4 broadcast_select_fusion.2
  95.1 4.6 %all-to-all-start.1 = ((bf16[8,128,512]{2,1,0:T(8,128)(2,1)}), bf16[8,128,512]{2,1,0:T(8,128)(2,1)}, u32[]{:S(2)}, u32[]{:S(2)}) async-start(bf16[8,128,512]{2,1,0:T(8,128)(2,1)} %broadcast_select_fusion.6), calls=%async_computation.1 | async-start | bytes 2097152 | tf_op jit(solution)/shard_map/all_to_all | solution.py:28
  99.7 2.5 fusion.47
  102.2 24.2 %all-to-all-done.1 = bf16[8,128,512]{2,1,0:T(8,128)(2,1)} async-done(((bf16[8,128,512]{2,1,0:T(8,128)(2,1)}), bf16[8,128,512]{2,1,0:T(8,128)(2,1)}, u32[]{:S(2)}, u32[]{:S(2)}) %all-to-all-start.1) | async-done | bytes 1048608 | tf_op jit(solution)/shard_map/all_to_all | solution.py:28
  126.4 2.5 pad_maximum_fusion.1
  128.9 13.2 %while.41 = (s32[]{:T(128)}, bf16[4,128,512]{2,1,0:T(8,128)(2,1)S(1)}, pred[4,4]{1,0:T(4,128)(4,1)S(1)}, bf16[4,4,128,128]{3,2,1,0:T(8,128)(2,1)}, s32[4,4]{1,0:...) while((s32[]{:T(128)}, bf16[4,128,512]{2,1,0:T(8,128)(2,1)S(1)}, pred[4,4]{1,0:T(4,128)(4,1)S(1)}, ...), condition=%wide.region_5.8_spmd, body=%wide.region_4.7_spmd.sunk | while | flops 67437592 | bytes 1972385 | solution.py:40
  129.0 2.0 gather_fusion.1
  132.2 2.0 gather_fusion.1
  134.3 1.2 fusion.79
  135.5 2.0 gather_fusion.1
  138.8 2.0 gather_fusion.1
  140.8 1.2 fusion.79
  142.1 1.9 fusion.54
  145.3 5.1 %gather_fusion.6 = bf16[1024,512]{1,0:T(8,128)(2,1)} fusion(bf16[512,512]{1,0:T(8,128)(2,1)S(1)} %maximum_convert_fusion.2, s32[1024]{0:T(1024)S(1)} %fusion.49), kind=kCustom, calls=%fused_computation.3.clone | custom fusion | bytes 2101248 | tf_op jit(solution)/shard_map/jit(_take)/gather | solution.py:23
  150.3 1.4 broadcast_select_fusion.1
  153.0 4.3 %all-to-all-start.2 = ((bf16[8,128,512]{2,1,0:T(8,128)(2,1)}), bf16[8,128,512]{2,1,0:T(8,128)(2,1)}, u32[]{:S(2)}, u32[]{:S(2)}) async-start(bf16[8,128,512]{2,1,0:T(8,128)(2,1)} %broadcast_select_fusion.5), calls=%async_computation.2 | async-start | bytes 2097152 | tf_op jit(solution)/shard_map/all_to_all | solution.py:28
  157.2 2.5 fusion.46
  159.7 24.1 %all-to-all-done.2 = bf16[8,128,512]{2,1,0:T(8,128)(2,1)} async-done(((bf16[8,128,512]{2,1,0:T(8,128)(2,1)}), bf16[8,128,512]{2,1,0:T(8,128)(2,1)}, u32[]{:S(2)}, u32[]{:S(2)}) %all-to-all-start.2) | async-done | bytes 1048608 | tf_op jit(solution)/shard_map/all_to_all | solution.py:28
  183.8 2.5 pad_maximum_fusion.2
  186.3 13.2 %while.42 = (s32[]{:T(128)}, bf16[4,128,512]{2,1,0:T(8,128)(2,1)S(1)}, pred[4,4]{1,0:T(4,128)(4,1)S(1)}, bf16[4,4,128,128]{3,2,1,0:T(8,128)(2,1)}, s32[4,4]{1,0:...) while((s32[]{:T(128)}, bf16[4,128,512]{2,1,0:T(8,128)(2,1)S(1)}, pred[4,4]{1,0:T(4,128)(4,1)S(1)}, ...), condition=%wide.region_9.12_spmd, body=%wide.region_8.11_spmd.sunk | while | flops 67437592 | bytes 1972385 | solution.py:40
  186.4 2.0 gather_fusion.2
  188.4 1.2 fusion.81
  189.7 2.0 gather_fusion.2
  193.0 2.0 gather_fusion.2
  196.2 2.0 gather_fusion.2
  198.3 1.2 fusion.81
  199.5 1.9 fusion.55
  202.7 5.1 %gather_fusion.7 = bf16[1024,512]{1,0:T(8,128)(2,1)} fusion(bf16[512,512]{1,0:T(8,128)(2,1)S(1)} %maximum_convert_fusion.1, s32[1024]{0:T(1024)S(1)} %fusion.49), kind=kCustom, calls=%fused_computation.4.clone | custom fusion | bytes 2101248 | tf_op jit(solution)/shard_map/jit(_take)/gather | solution.py:23
  207.8 1.4 broadcast_select_fusion
  210.4 4.2 %all-to-all-start.3 = ((bf16[8,128,512]{2,1,0:T(8,128)(2,1)}), bf16[8,128,512]{2,1,0:T(8,128)(2,1)}, u32[]{:S(2)}, u32[]{:S(2)}) async-start(bf16[8,128,512]{2,1,0:T(8,128)(2,1)} %broadcast_select_fusion.4), calls=%async_computation.3 | async-start | bytes 2097152 | tf_op jit(solution)/shard_map/all_to_all | solution.py:28
  214.7 2.5 fusion.64
  219.3 2.5 fusion.45
  221.8 19.4 %all-to-all-done.3 = bf16[8,128,512]{2,1,0:T(8,128)(2,1)} async-done(((bf16[8,128,512]{2,1,0:T(8,128)(2,1)}), bf16[8,128,512]{2,1,0:T(8,128)(2,1)}, u32[]{:S(2)}, u32[]{:S(2)}) %all-to-all-start.3) | async-done | bytes 1048608 | tf_op jit(solution)/shard_map/all_to_all | solution.py:28
  241.2 2.5 pad_maximum_fusion.3
  243.8 13.2 %while.43 = (s32[]{:T(128)}, bf16[4,128,512]{2,1,0:T(8,128)(2,1)S(1)}, pred[4,4]{1,0:T(4,128)(4,1)S(1)}, bf16[4,4,128,128]{3,2,1,0:T(8,128)(2,1)}, s32[4,4]{1,0:...) while((s32[]{:T(128)}, bf16[4,128,512]{2,1,0:T(8,128)(2,1)S(1)}, pred[4,4]{1,0:T(4,128)(4,1)S(1)}, ...), condition=%wide.region_13.16_spmd, body=%wide.region_12.15_spmd.sunk | while | flops 67437592 | bytes 1972385 | solution.py:40
  243.8 2.0 gather_fusion.3
  247.1 2.0 gather_fusion.3
  250.4 2.0 gather_fusion.3
  252.4 1.2 fusion.83
  253.7 2.0 gather_fusion.3
  256.9 1.9 fusion.56
  260.5 27.8 %all_to_all.32 = bf16[4,1,512,512]{3,2,1,0:T(8,128)(2,1)S(1)} all-to-all(bf16[4,1,512,512]{3,2,1,0:T(8,128)(2,1)S(1)} %maximum_bitcast_fusion), channel_id=1, replica_groups=mesh['segment'=4,'dom'=8] {'segment'}, dimensions={0} | all-to-all | bytes 4194304 | tf_op jit(solution)/shard_map/all_to_all | solution.py:84
  288.3 1.3 copy.49
  (122 shorter events, 27.5 us)
Async XLA Ops:
  6.5 1.6 copy-start
  6.5 63.0 %all-gather.5.cloned.1.call-start = ((), (), s32[]{:S(2)}) async-start(), calls=%async_computation.5 | async-start | bytes 2621440 | tf_op jit(solution)/shard_map/all_gather | solution.py:61
  16.1 8.4 %copy-start.10 = (bf16[1,512]{1,0:T(2,128)(2,1)S(1)}, bf16[1,512]{1,0:T(2,128)(2,1)}, u32[]{:S(2)}) copy-start(bf16[1,512]{1,0:T(2,128)(2,1)} %param.30) | copy-start | bytes 3076
  17.3 16.9 %copy-start.11 = (bf16[1,512]{1,0:T(2,128)(2,1)S(1)}, bf16[1,512]{1,0:T(2,128)(2,1)}, u32[]{:S(2)}) copy-start(bf16[1,512]{1,0:T(2,128)(2,1)} %param.31) | copy-start | bytes 3076
  17.3 33.2 %all-to-all-start = ((bf16[8,128,512]{2,1,0:T(8,128)(2,1)}), bf16[8,128,512]{2,1,0:T(8,128)(2,1)}, u32[]{:S(2)}, u32[]{:S(2)}) async-start(bf16[8,128,512]{2,1,0:T(8,128)(2,1)} %broadcast_select_fusion.7), calls=%async_computation | async-start | bytes 2097152 | tf_op jit(solution)/shard_map/all_to_all | solution.py:28
  23.8 60.4 %all-gather.7.cloned.1.call-start = ((), (), s32[]{:S(2)}) async-start(), calls=%async_computation.6 | async-start | bytes 2621440 | tf_op jit(solution)/shard_map/all_gather | solution.py:62
  69.5 14.7 %copy-start.6 = (bf16[4,128,512]{2,1,0:T(8,128)(2,1)S(1)}, bf16[4,128,512]{2,1,0:T(8,128)(2,1)}, u32[]{:S(2)}) copy-start(bf16[4,128,512]{2,1,0:T(8,128)(2,1)} %get-tuple-element.135) | copy-start | bytes 1572868
  86.1 1.0 copy-start.1
  95.1 31.3 %all-to-all-start.1 = ((bf16[8,128,512]{2,1,0:T(8,128)(2,1)}), bf16[8,128,512]{2,1,0:T(8,128)(2,1)}, u32[]{:S(2)}, u32[]{:S(2)}) async-start(bf16[8,128,512]{2,1,0:T(8,128)(2,1)} %broadcast_select_fusion.6), calls=%async_computation.1 | async-start | bytes 2097152 | tf_op jit(solution)/shard_map/all_to_all | solution.py:28
  144.0 1.0 copy-start.2
  153.0 30.8 %all-to-all-start.2 = ((bf16[8,128,512]{2,1,0:T(8,128)(2,1)}), bf16[8,128,512]{2,1,0:T(8,128)(2,1)}, u32[]{:S(2)}, u32[]{:S(2)}) async-start(bf16[8,128,512]{2,1,0:T(8,128)(2,1)} %broadcast_select_fusion.5), calls=%async_computation.2 | async-start | bytes 2097152 | tf_op jit(solution)/shard_map/all_to_all | solution.py:28
  201.4 1.0 copy-start.4
  210.4 30.8 %all-to-all-start.3 = ((bf16[8,128,512]{2,1,0:T(8,128)(2,1)}), bf16[8,128,512]{2,1,0:T(8,128)(2,1)}, u32[]{:S(2)}, u32[]{:S(2)}) async-start(bf16[8,128,512]{2,1,0:T(8,128)(2,1)} %broadcast_select_fusion.4), calls=%async_computation.3 | async-start | bytes 2097152 | tf_op jit(solution)/shard_map/all_to_all | solution.py:28
  214.7 2.5 copy-start.3
  214.7 3.6 %copy-start.5 = (f32[512,512]{1,0:T(8,128)S(1)}, f32[512,512]{1,0:T(8,128)}, u32[]{:S(2)}) copy-start(f32[512,512]{1,0:T(8,128)} %copy-done.4) | copy-start | bytes 3145732
  258.9 1.0 copy-start.7
  258.9 1.2 copy-start.8
  258.9 1.3 copy-start.9
Sparse Core Ops, SparseCore 0:
  9.2 37.9 all-gather.4
  49.0 35.1 all-gather.6
where the time goes:
time: 298 us; the launch traced here: 296 us
  waiting for transfers between devices  87.4 us (29%)
  local copies, waits for them, and re-layouts  61.9 us (21%)
  blocking collectives  44.2 us (15%)
  matrix products  39.7 us (13%)
  other arithmetic  29.3 us (10%)
  starting transfers between devices  19.6 us (7%)
  between operations  13.7 us (5%)
    all_to_all x4, waiting for transfers between devices, sage_layer(): lax.all_to_all(outgoing, 'dom', split_axis=0, concat_axis=0, tiled=True)  73.8 us
    gather x16, local copies, waits for them, and re-layouts, block_sum(): chosen = jnp.take(sources, block_index, axis=0)  31.8 us
    all_to_all x1, blocking collectives, per_device(): lax.all_to_all(dealt_out, 'segment', split_axis=0, concat_axis=1, tiled=T...  27.8 us
    dot_general x16, matrix products, block_sum(): jnp.einsum('kij,kjd->id', masked, chosen, preferred_element_type=jnp.floa...  22.2 us
    gather x4, local copies, waits for them, and re-layouts, sage_layer(): jnp.take(inputs, send_list.reshape(-1), axis=0)  20.3 us
    all_to_all x4, starting transfers between devices, sage_layer(): lax.all_to_all(outgoing, 'dom', split_axis=0, concat_axis=0, tiled=True)  19.6 us
    all_gather x1, waiting for transfers between devices, per_device(): lax.all_gather(w_neigh, 'segment', axis=0, tiled=True)  12.2 us
    concatenate x4, other arithmetic, sage_layer(): jnp.concatenate([inputs.reshape(block_count, tile_rows, feat_width), inco...  10 us
  transfers between devices with their start and end apart: 6, of which 5 were waited for; matrix products, arithmetic and copies ran while one was open for 16% of the time, Pallas kernels for 0%

commit v1 on v0

--- a/solution.py
+++ b/solution.py
@@ -4,6 +4,18 @@
 from jax.sharding import PartitionSpec as P
 
 norm_eps = 1e-05
+
+
+def rotated_exchange(array, axis, split, join):
+    ways, here = (lax.axis_size(axis), lax.axis_index(axis))
+    width = array.shape[split] // ways
+    turned = jnp.roll(array, -here * width, axis=split)
+    got = [lax.slice_in_dim(turned, 0, width, axis=split)]
+    for far in range(1, ways):
+        sent = lax.slice_in_dim(turned, far * width, (far + 1) * width, axis=split)
+        got.append(lax.ppermute(sent, axis, [(d, (d + far) % ways) for d in range(ways)]))
+    line = jnp.concatenate(got[::-1], axis=join)
+    return jnp.roll(line, (here + 1) * got[0].shape[join], axis=join)
 
 
 def select_span(array_in, span_id):
@@ -25,7 +37,7 @@
     )
     row_live = lax.broadcasted_iota(jnp.int32, (peer_count, tile_rows), 1) < send_count[:, None]
     outgoing = jnp.where(row_live[:, :, None], picked, jnp.zeros_like(picked))
-    incoming = lax.all_to_all(outgoing, "dom", split_axis=0, concat_axis=0, tiled=True)
+    incoming = rotated_exchange(outgoing, "dom", 0, 0)
     sources = jnp.concatenate(
         [inputs.reshape(block_count, tile_rows, feat_width), incoming], axis=0
     )

time: 298 us -> 258 us (0.87)
  local copies, waits for them, and re-layouts: 61.9 us -> 44.1 us
  waiting for transfers between devices: 87.4 us -> 71.6 us
  other arithmetic: 29.3 us -> 15.8 us
  starting transfers between devices: 19.6 us -> 28.3 us
    all_to_all x4 -> x0, waiting for transfers between devices: 73.8 us -> none  [sage_layer(): lax.all_to_all(outgoing, 'dom', split_axis=0, concat_axis=0, tiled=True)]
    ppermute x0 -> x28, waiting for transfers between devices: none -> 53.3 us  [rotated_exchange(): lax.ppermute(sent, axis, [(d, (d + far) % ways) for d in range(ways)])]
    ppermute x0 -> x28, starting transfers between devices: none -> 28.3 us  [rotated_exchange(): lax.ppermute(sent, axis, [(d, (d + far) % ways) for d in range(ways)])]
    gather x16, local copies, waits for them, and re-layouts: 31.8 us -> 9.29 us  [block_sum(): chosen = jnp.take(sources, block_index, axis=0)]
    all_to_all x4 -> x0, starting transfers between devices: 19.6 us -> none  [sage_layer(): lax.all_to_all(outgoing, 'dom', split_axis=0, concat_axis=0, tiled=True)]
    concatenate x4, other arithmetic: 10 us -> 0.56 us  [sage_layer(): jnp.concatenate([inputs.reshape(block_count, tile_rows, feat_width), inco...]
    unnamed x25 -> x71, local copies, waits for them, and re-layouts: 4.51 us -> 11.5 us
    all_gather x1, waiting for transfers between devices: 12.2 us -> 17.6 us  [per_device(): lax.all_gather(w_neigh, 'segment', axis=0, tiled=True)]
  transfers between devices with their start and end apart: 6 -> 30, of which waited for: 5 -> 10; matrix products, arithmetic and copies ran while one was open for 16% -> 16% of each run, Pallas kernels for 0% -> 0%
where the time goes in v1:
time: 258 us; the launch traced here: 257 us
  waiting for transfers between devices  71.6 us (28%)
  local copies, waits for them, and re-layouts  44.1 us (17%)
  blocking collectives  43.4 us (17%)
  matrix products  38.7 us (15%)
  starting transfers between devices  28.3 us (11%)
  other arithmetic  15.8 us (6%)
  between operations  14.2 us (6%)
    ppermute x28, waiting for transfers between devices, rotated_exchange(): lax.ppermute(sent, axis, [(d, (d + far) % ways) for d in range(ways)])  53.3 us
    ppermute x28, starting transfers between devices, rotated_exchange(): lax.ppermute(sent, axis, [(d, (d + far) % ways) for d in range(ways)])  28.3 us
    all_to_all x1, blocking collectives, per_device(): lax.all_to_all(dealt_out, 'segment', split_axis=0, concat_axis=1, tiled=T...  27 us
    dot_general x16, matrix products, block_sum(): jnp.einsum('kij,kjd->id', masked, chosen, preferred_element_type=jnp.floa...  22.1 us
    all_gather x1, waiting for transfers between devices, per_device(): lax.all_gather(w_neigh, 'segment', axis=0, tiled=True)  17.6 us
    gather x4, local copies, waits for them, and re-layouts, sage_layer(): jnp.take(inputs, send_list.reshape(-1), axis=0)  17 us
    unnamed x71, local copies, waits for them, and re-layouts  11.5 us
    gather x16, local copies, waits for them, and re-layouts, block_sum(): chosen = jnp.take(sources, block_index, axis=0)  9.29 us
  transfers between devices with their start and end apart: 30, of which 10 were waited for; matrix products, arithmetic and copies ran while one was open for 16% of the time, Pallas kernels for 0%

profile of v1, /device:TPU:0, one launch (start us, length us, event | category | flops | bytes accessed | tf_op | source)
XLA Modules:
  0.0 256.8 jit_solution(874917755869917481)
XLA Ops:
  8.2 5.1 %gather_fusion.4 = bf16[1024,512]{1,0:T(8,128)(2,1)} fusion(bf16[512,512]{1,0:T(8,128)(2,1)S(1)} %fusion.81, s32[1024]{0:T(1024)S(1)} %fusion.58), kind=kCustom, calls=%fused_computation.clone | custom fusion | bytes 2101248 | tf_op jit(solution)/shard_map/jit(_take)/gather | solution.py:35
  14.7 1.4 broadcast_select_fusion.3
  16.7 1.0 copy-done.2
  17.8 4.6 %collective-permute-start = (bf16[1,128,512]{2,1,0:T(8,128)(2,1)S(1)}, bf16[1,128,512]{2,1,0:T(8,128)(2,1)}, u32[]{:S(2)}, u32[]{:S(2)}) collective-permute-start(bf16[1,128,512]{2,1,0:T(8,128)(2,1)S(1)} %get-tuple-element.223), channel_id=1, source_target_pairs={{0,7},{1,0},{2,1},{3,2},{4,3},{5,4},{6,5},{7,6},{8,15},{9,8},{10,9... | collective-permute-start | bytes 393224 | tf_op jit(solution)/shard_map/ppermute | solution.py:16
  23.0 2.7 %collective-permute-start.3 = (bf16[1,128,512]{2,1,0:T(8,128)(2,1)S(1)}, bf16[1,128,512]{2,1,0:T(8,128)(2,1)}, u32[]{:S(2)}, u32[]{:S(2)}) collective-permute-start(bf16[1,128,512]{2,1,0:T(8,128)(2,1)S(1)} %get-tuple-element.220), channel_id=1, source_target_pairs={{0,4},{1,5},{2,6},{3,7},{4,0},{5,1},{6,2},{7,3},{8,12},{9,13},{10,... | collective-permute-start | bytes 393224 | tf_op jit(solution)/shard_map/ppermute | solution.py:16
  27.0 8.1 %all-gather = bf16[4,1,512]{2,1,0:T(2,128)(2,1)S(1)} all-gather(bf16[1,1,512]{2,1,0:T(2,128)(2,1)S(1)} %bitcast.205), channel_id=1, replica_groups=mesh['segment'=4,'dom'=8] {'segment'}, dimensions={0}, use_global_device_ids=true | all-gather | bytes 5120 | tf_op jit(solution)/shard_map/all_gather | solution.py:75
  35.7 8.4 %all-gather.1 = bf16[4,1,512]{2,1,0:T(2,128)(2,1)S(1)} all-gather(bf16[1,1,512]{2,1,0:T(2,128)(2,1)} %bitcast.206), channel_id=1, replica_groups=mesh['segment'=4,'dom'=8] {'segment'}, dimensions={0}, use_global_device_ids=true | all-gather | bytes 5120 | tf_op jit(solution)/shard_map/all_gather | solution.py:76
  44.7 1.9 dynamic-slice_bitcast_fusion.4
  49.0 0.9 constant_dynamic-update-slice_fusion.5
  49.9 0.9 constant_dynamic-update-slice_fusion.4
  50.8 0.9 constant_dynamic-update-slice_fusion.3
  52.7 1.7 collective-permute-done.5
  54.4 1.1 collective-permute-done.6
  55.5 0.9 slice_dynamic-update-slice_fusion.3
  57.5 7.5 %while.40 = (s32[]{:T(128)}, bf16[4,128,512]{2,1,0:T(8,128)(2,1)S(1)}, pred[4,4]{1,0:T(4,128)(4,1)S(1)}, bf16[4,4,128,128]{3,2,1,0:T(8,128)(2,1)}, s32[4,4]{1,0:...) while((s32[]{:T(128)}, bf16[4,128,512]{2,1,0:T(8,128)(2,1)S(1)}, pred[4,4]{1,0:T(4,128)(4,1)S(1)}, ...), condition=%wide.region_1.5_spmd, body=%wide.region_0.4_spmd.sunk | while | flops 67437592 | bytes 1972385 | solution.py:52
  58.1 1.2 fusion.91
  60.0 1.2 fusion.91
  61.9 1.2 fusion.91
  63.7 1.2 fusion.91
  65.0 1.6 fusion.56
  66.7 17.6 %all-gather.7.cloned.1.call-done = bf16[4,512,512]{2,1,0:T(8,128)(2,1)} async-done(((bf16[1,512,512]{2,1,0:T(8,128)(2,1)}), bf16[4,512,512]{2,1,0:T(8,128)(2,1)}) %all-gather.7.cloned.1.call-update) | async-done | bytes 2097168 | tf_op jit(solution)/shard_map/all_gather | solution.py:74
  84.2 1.7 fusion.67
  86.5 4.0 %gather_fusion.5 = bf16[1024,512]{1,0:T(8,128)(2,1)S(1)} fusion(bf16[512,512]{1,0:T(8,128)(2,1)S(1)} %maximum_convert_fusion.3, s32[1024]{0:T(1024)S(1)} %fusion.58), kind=kCustom, calls=%fused_computation.2.clone | custom fusion | bytes 2101248 | tf_op jit(solution)/shard_map/jit(_take)/gather | solution.py:35
  91.8 2.7 %collective-permute-start.7 = (bf16[1,128,512]{2,1,0:T(8,128)(2,1)S(1)}, bf16[1,128,512]{2,1,0:T(8,128)(2,1)S(1)}, u32[]{:S(2)}, u32[]{:S(2)}) collective-permute-start(bf16[1,128,512]{2,1,0:T(8,128)(2,1)S(1)} %get-tuple-element.216), channel_id=1, source_target_pairs={{0,7},{1,0},{2,1},{3,2},{4,3},{5,4},{6,5},{7,6},{8,15},{9,8},{10,9... | collective-permute-start | bytes 393224 | tf_op jit(solution)/shard_map/ppermute | solution.py:16
  95.3 2.4 fusion.55
  97.7 1.1 fusion.78
  98.8 2.7 %collective-permute-start.10 = (bf16[1,128,512]{2,1,0:T(8,128)(2,1)S(1)}, bf16[1,128,512]{2,1,0:T(8,128)(2,1)S(1)}, u32[]{:S(2)}, u32[]{:S(2)}) collective-permute-start(bf16[1,128,512]{2,1,0:T(8,128)(2,1)S(1)} %get-tuple-element.213), channel_id=1, source_target_pairs={{0,4},{1,5},{2,6},{3,7},{4,0},{5,1},{6,2},{7,3},{8,12},{9,13},{10,... | collective-permute-start | bytes 393224 | tf_op jit(solution)/shard_map/ppermute | solution.py:16
  103.3 15.7 %collective-permute-done.10 = bf16[1,128,512]{2,1,0:T(8,128)(2,1)S(1)} collective-permute-done((bf16[1,128,512]{2,1,0:T(8,128)(2,1)S(1)}, bf16[1,128,512]{2,1,0:T(8,128)(2,1)S(1)}, u32[]{:S(2)}, u32[]{:S(2)}) %collective-permute-start.10) | collective-permute-done | bytes 131104 | tf_op jit(solution)/shard_map/ppermute | solution.py:16
  119.0 1.1 collective-permute-done.11
  120.8 7.5 %while.41 = (s32[]{:T(128)}, bf16[4,128,512]{2,1,0:T(8,128)(2,1)S(1)}, pred[4,4]{1,0:T(4,128)(4,1)S(1)}, bf16[4,4,128,128]{3,2,1,0:T(8,128)(2,1)}, s32[4,4]{1,0:...) while((s32[]{:T(128)}, bf16[4,128,512]{2,1,0:T(8,128)(2,1)S(1)}, pred[4,4]{1,0:T(4,128)(4,1)S(1)}, ...), condition=%wide.region_5.9_spmd, body=%wide.region_4.8_spmd.sunk | while | flops 67437592 | bytes 1972385 | solution.py:52
  121.4 1.2 fusion.93
  123.3 1.2 fusion.93
  125.2 1.2 fusion.93
  127.0 1.2 fusion.93
  129.1 2.1 fusion.68
  131.7 4.0 %gather_fusion.6 = bf16[1024,512]{1,0:T(8,128)(2,1)S(1)} fusion(bf16[512,512]{1,0:T(8,128)(2,1)S(1)} %maximum_convert_fusion.2, s32[1024]{0:T(1024)S(1)} %fusion.58), kind=kCustom, calls=%fused_computation.3.clone | custom fusion | bytes 2101248 | tf_op jit(solution)/shard_map/jit(_take)/gather | solution.py:35
  137.4 2.4 fusion.54
  139.8 1.1 fusion.79
  141.6 1.6 collective-permute-start.17
  143.2 2.7 %collective-permute-start.19 = (bf16[1,128,512]{2,1,0:T(8,128)(2,1)S(1)}, bf16[1,128,512]{2,1,0:T(8,128)(2,1)S(1)}, u32[]{:S(2)}, u32[]{:S(2)}) collective-permute-start(bf16[1,128,512]{2,1,0:T(8,128)(2,1)S(1)} %get-tuple-element.204), channel_id=1, source_target_pairs={{0,2},{1,3},{2,4},{3,5},{4,6},{5,7},{6,0},{7,1},{8,10},{9,11},{10,... | collective-permute-start | bytes 393224 | tf_op jit(solution)/shard_map/ppermute | solution.py:16
  146.4 15.2 %collective-permute-done.17 = bf16[1,128,512]{2,1,0:T(8,128)(2,1)S(1)} collective-permute-done((bf16[1,128,512]{2,1,0:T(8,128)(2,1)S(1)}, bf16[1,128,512]{2,1,0:T(8,128)(2,1)S(1)}, u32[]{:S(2)}, u32[]{:S(2)}) %collective-permute-start.17) | collective-permute-done | bytes 131104 | tf_op jit(solution)/shard_map/ppermute | solution.py:16
  161.6 1.3 collective-permute-done.18
  163.6 7.5 %while.42 = (s32[]{:T(128)}, bf16[4,128,512]{2,1,0:T(8,128)(2,1)S(1)}, pred[4,4]{1,0:T(4,128)(4,1)S(1)}, bf16[4,4,128,128]{3,2,1,0:T(8,128)(2,1)}, s32[4,4]{1,0:...) while((s32[]{:T(128)}, bf16[4,128,512]{2,1,0:T(8,128)(2,1)S(1)}, pred[4,4]{1,0:T(4,128)(4,1)S(1)}, ...), condition=%wide.region_9.13_spmd, body=%wide.region_8.12_spmd.sunk | while | flops 67437592 | bytes 1972385 | solution.py:52
  164.3 1.2 fusion.95
  166.2 1.2 fusion.95
  168.1 1.2 fusion.95
  169.9 1.2 fusion.95
  172.0 2.1 fusion.69
  174.6 4.0 %gather_fusion.7 = bf16[1024,512]{1,0:T(8,128)(2,1)S(1)} fusion(bf16[512,512]{1,0:T(8,128)(2,1)S(1)} %maximum_convert_fusion.1, s32[1024]{0:T(1024)S(1)} %fusion.58), kind=kCustom, calls=%fused_computation.4.clone | custom fusion | bytes 2101248 | tf_op jit(solution)/shard_map/jit(_take)/gather | solution.py:35
  180.2 2.4 fusion.53
  182.7 1.1 fusion.80
  184.4 1.7 collective-permute-start.24
  186.3 2.4 collective-permute-start.26
  189.0 15.5 %collective-permute-done.24 = bf16[1,128,512]{2,1,0:T(8,128)(2,1)S(1)} collective-permute-done((bf16[1,128,512]{2,1,0:T(8,128)(2,1)S(1)}, bf16[1,128,512]{2,1,0:T(8,128)(2,1)S(1)}, u32[]{:S(2)}, u32[]{:S(2)}) %collective-permute-start.24) | collective-permute-done | bytes 131104 | tf_op jit(solution)/shard_map/ppermute | solution.py:16
  204.5 1.3 collective-permute-done.25
  207.3 10.0 %while.43 = (s32[]{:T(128)}, bf16[4,128,512]{2,1,0:T(8,128)(2,1)}, pred[4,4]{1,0:T(4,128)(4,1)S(1)}, bf16[4,4,128,128]{3,2,1,0:T(8,128)(2,1)}, s32[4,4]{1,0:T(4,...) while((s32[]{:T(128)}, bf16[4,128,512]{2,1,0:T(8,128)(2,1)}, pred[4,4]{1,0:T(4,128)(4,1)S(1)}, ...), condition=%wide.region_13.17_spmd, body=%wide.region_12.16_spmd.sunk | while | flops 67437592 | bytes 1971369 | solution.py:52
  207.9 1.9 fusion.97
  210.4 1.9 fusion.97
  212.9 1.9 fusion.97
  215.4 1.9 fusion.97
  217.3 1.7 fusion.70
  220.7 27.0 %all_to_all.12 = bf16[4,1,512,512]{3,2,1,0:T(8,128)(2,1)S(1)} all-to-all(bf16[4,1,512,512]{3,2,1,0:T(8,128)(2,1)S(1)} %maximum_bitcast_fusion), channel_id=1, replica_groups=mesh['segment'=4,'dom'=8] {'segment'}, dimensions={0} | all-to-all | bytes 4194304 | tf_op jit(solution)/shard_map/all_to_all | solution.py:96
  247.6 1.3 copy.77
  248.9 1.0 copy-done.1
  (232 shorter events, 37.7 us)
Async XLA Ops:
  6.5 1.6 copy-start
  6.5 58.5 %all-gather.5.cloned.1.call-start = ((), (), s32[]{:S(2)}) async-start(), calls=%async_computation.1 | async-start | bytes 2621440 | tf_op jit(solution)/shard_map/all_gather | solution.py:73
  7.3 77.0 %all-gather.7.cloned.1.call-start = ((), (), s32[]{:S(2)}) async-start(), calls=%async_computation.2 | async-start | bytes 2621440 | tf_op jit(solution)/shard_map/all_gather | solution.py:74
  14.7 1.7 copy-start.15
  16.7 1.0 copy-start.2
  17.7 9.3 %copy-start.19 = (bf16[1,512]{1,0:T(2,128)(2,1)S(1)}, bf16[1,512]{1,0:T(2,128)(2,1)}, u32[]{:S(2)}) copy-start(bf16[1,512]{1,0:T(2,128)(2,1)} %param.32) | copy-start | bytes 3076
  17.8 29.5 %collective-permute-start = (bf16[1,128,512]{2,1,0:T(8,128)(2,1)S(1)}, bf16[1,128,512]{2,1,0:T(8,128)(2,1)}, u32[]{:S(2)}, u32[]{:S(2)}) collective-permute-start(bf16[1,128,512]{2,1,0:T(8,128)(2,1)S(1)} %get-tuple-element.223), channel_id=1, source_target_pairs={{0,7},{1,0},{2,1},{3,2},{4,3},{5,4},{6,5},{7,6},{8,15},{9,8},{10,9... | collective-permute-start | bytes 393224 | tf_op jit(solution)/shard_map/ppermute | solution.py:16
  22.3 26.6 %collective-permute-start.1 = (bf16[1,128,512]{2,1,0:T(8,128)(2,1)S(1)}, bf16[1,128,512]{2,1,0:T(8,128)(2,1)}, u32[]{:S(2)}, u32[]{:S(2)}) collective-permute-start(bf16[1,128,512]{2,1,0:T(8,128)(2,1)S(1)} %get-tuple-element.222), channel_id=1, source_target_pairs={{0,6},{1,7},{2,0},{3,1},{4,2},{5,3},{6,4},{7,5},{8,14},{9,15},{10,... | collective-permute-start | bytes 393224 | tf_op jit(solution)/shard_map/ppermute | solution.py:16
  23.0 26.9 %collective-permute-start.2 = (bf16[1,128,512]{2,1,0:T(8,128)(2,1)S(1)}, bf16[1,128,512]{2,1,0:T(8,128)(2,1)}, u32[]{:S(2)}, u32[]{:S(2)}) collective-permute-start(bf16[1,128,512]{2,1,0:T(8,128)(2,1)S(1)} %get-tuple-element.221), channel_id=1, source_target_pairs={{0,5},{1,6},{2,7},{3,0},{4,1},{5,2},{6,3},{7,4},{8,13},{9,14},{10,... | collective-permute-start | bytes 393224 | tf_op jit(solution)/shard_map/ppermute | solution.py:16
  23.0 27.9 %collective-permute-start.3 = (bf16[1,128,512]{2,1,0:T(8,128)(2,1)S(1)}, bf16[1,128,512]{2,1,0:T(8,128)(2,1)}, u32[]{:S(2)}, u32[]{:S(2)}) collective-permute-start(bf16[1,128,512]{2,1,0:T(8,128)(2,1)S(1)} %get-tuple-element.220), channel_id=1, source_target_pairs={{0,4},{1,5},{2,6},{3,7},{4,0},{5,1},{6,2},{7,3},{8,12},{9,13},{10,... | collective-permute-start | bytes 393224 | tf_op jit(solution)/shard_map/ppermute | solution.py:16
  25.7 26.1 %collective-permute-start.4 = (bf16[1,128,512]{2,1,0:T(8,128)(2,1)S(1)}, bf16[1,128,512]{2,1,0:T(8,128)(2,1)}, u32[]{:S(2)}, u32[]{:S(2)}) collective-permute-start(bf16[1,128,512]{2,1,0:T(8,128)(2,1)S(1)} %get-tuple-element.219), channel_id=1, source_target_pairs={{0,3},{1,4},{2,5},{3,6},{4,7},{5,0},{6,1},{7,2},{8,11},{9,12},{10,... | collective-permute-start | bytes 393224 | tf_op jit(solution)/shard_map/ppermute | solution.py:16
  47.3 7.1 %collective-permute-start.5 = (bf16[1,128,512]{2,1,0:T(8,128)(2,1)S(1)}, bf16[1,128,512]{2,1,0:T(8,128)(2,1)S(1)}, u32[]{:S(2)}, u32[]{:S(2)}) collective-permute-start(bf16[1,128,512]{2,1,0:T(8,128)(2,1)S(1)} %get-tuple-element.218), channel_id=1, source_target_pairs={{0,2},{1,3},{2,4},{3,5},{4,6},{5,7},{6,0},{7,1},{8,10},{9,11},{10,... | collective-permute-start | bytes 393224 | tf_op jit(solution)/shard_map/ppermute | solution.py:16
  48.9 6.6 %collective-permute-start.6 = (bf16[1,128,512]{2,1,0:T(8,128)(2,1)S(1)}, bf16[1,128,512]{2,1,0:T(8,128)(2,1)S(1)}, u32[]{:S(2)}, u32[]{:S(2)}) collective-permute-start(bf16[1,128,512]{2,1,0:T(8,128)(2,1)S(1)} %get-tuple-element.217), channel_id=1, source_target_pairs={{0,1},{1,2},{2,3},{3,4},{4,5},{5,6},{6,7},{7,0},{8,9},{9,10},{10,1... | collective-permute-start | bytes 393224 | tf_op jit(solution)/shard_map/ppermute | solution.py:16
  56.8 0.6 copy-start.20
  65.0 19.3 %copy-start.4 = (bf16[4,128,512]{2,1,0:T(8,128)(2,1)}, bf16[4,128,512]{2,1,0:T(8,128)(2,1)S(1)}, u32[]{:S(2)}) copy-start(bf16[4,128,512]{2,1,0:T(8,128)(2,1)S(1)} %get-tuple-element.136) | copy-start | bytes 1572868
  84.2 2.0 copy-start.13
  84.2 2.0 copy-start.14
  90.5 0.6 copy-start.16
  91.8 9.7 %collective-permute-start.7 = (bf16[1,128,512]{2,1,0:T(8,128)(2,1)S(1)}, bf16[1,128,512]{2,1,0:T(8,128)(2,1)S(1)}, u32[]{:S(2)}, u32[]{:S(2)}) collective-permute-start(bf16[1,128,512]{2,1,0:T(8,128)(2,1)S(1)} %get-tuple-element.216), channel_id=1, source_target_pairs={{0,7},{1,0},{2,1},{3,2},{4,3},{5,4},{6,5},{7,6},{8,15},{9,8},{10,9... | collective-permute-start | bytes 393224 | tf_op jit(solution)/shard_map/ppermute | solution.py:16
  94.5 7.8 %collective-permute-start.8 = (bf16[1,128,512]{2,1,0:T(8,128)(2,1)S(1)}, bf16[1,128,512]{2,1,0:T(8,128)(2,1)S(1)}, u32[]{:S(2)}, u32[]{:S(2)}) collective-permute-start(bf16[1,128,512]{2,1,0:T(8,128)(2,1)S(1)} %get-tuple-element.215), channel_id=1, source_target_pairs={{0,6},{1,7},{2,0},{3,1},{4,2},{5,3},{6,4},{7,5},{8,14},{9,15},{10,... | collective-permute-start | bytes 393224 | tf_op jit(solution)/shard_map/ppermute | solution.py:16
  98.8 4.4 %collective-permute-start.9 = (bf16[1,128,512]{2,1,0:T(8,128)(2,1)S(1)}, bf16[1,128,512]{2,1,0:T(8,128)(2,1)S(1)}, u32[]{:S(2)}, u32[]{:S(2)}) collective-permute-start(bf16[1,128,512]{2,1,0:T(8,128)(2,1)S(1)} %get-tuple-element.214), channel_id=1, source_target_pairs={{0,5},{1,6},{2,7},{3,0},{4,1},{5,2},{6,3},{7,4},{8,13},{9,14},{10,... | collective-permute-start | bytes 393224 | tf_op jit(solution)/shard_map/ppermute | solution.py:16
  98.8 20.1 %collective-permute-start.10 = (bf16[1,128,512]{2,1,0:T(8,128)(2,1)S(1)}, bf16[1,128,512]{2,1,0:T(8,128)(2,1)S(1)}, u32[]{:S(2)}, u32[]{:S(2)}) collective-permute-start(bf16[1,128,512]{2,1,0:T(8,128)(2,1)S(1)} %get-tuple-element.213), channel_id=1, source_target_pairs={{0,4},{1,5},{2,6},{3,7},{4,0},{5,1},{6,2},{7,3},{8,12},{9,13},{10,... | collective-permute-start | bytes 393224 | tf_op jit(solution)/shard_map/ppermute | solution.py:16
  101.5 18.6 %collective-permute-start.11 = (bf16[1,128,512]{2,1,0:T(8,128)(2,1)S(1)}, bf16[1,128,512]{2,1,0:T(8,128)(2,1)S(1)}, u32[]{:S(2)}, u32[]{:S(2)}) collective-permute-start(bf16[1,128,512]{2,1,0:T(8,128)(2,1)S(1)} %get-tuple-element.212), channel_id=1, source_target_pairs={{0,3},{1,4},{2,5},{3,6},{4,7},{5,0},{6,1},{7,2},{8,11},{9,12},{10,... | collective-permute-start | bytes 393224 | tf_op jit(solution)/shard_map/ppermute | solution.py:16
  101.5 18.6 %collective-permute-start.12 = (bf16[1,128,512]{2,1,0:T(8,128)(2,1)S(1)}, bf16[1,128,512]{2,1,0:T(8,128)(2,1)S(1)}, u32[]{:S(2)}, u32[]{:S(2)}) collective-permute-start(bf16[1,128,512]{2,1,0:T(8,128)(2,1)S(1)} %get-tuple-element.211), channel_id=1, source_target_pairs={{0,2},{1,3},{2,4},{3,5},{4,6},{5,7},{6,0},{7,1},{8,10},{9,11},{10,... | collective-permute-start | bytes 393224 | tf_op jit(solution)/shard_map/ppermute | solution.py:16
  102.3 17.8 %collective-permute-start.13 = (bf16[1,128,512]{2,1,0:T(8,128)(2,1)S(1)}, bf16[1,128,512]{2,1,0:T(8,128)(2,1)S(1)}, u32[]{:S(2)}, u32[]{:S(2)}) collective-permute-start(bf16[1,128,512]{2,1,0:T(8,128)(2,1)S(1)} %get-tuple-element.210), channel_id=1, source_target_pairs={{0,1},{1,2},{2,3},{3,4},{4,5},{5,6},{6,7},{7,0},{8,9},{9,10},{10,1... | collective-permute-start | bytes 393224 | tf_op jit(solution)/shard_map/ppermute | solution.py:16
  128.3 0.8 copy-start.5
  129.1 2.4 copy-start.11
  129.1 2.4 copy-start.12
  136.6 6.6 %collective-permute-start.14 = (bf16[1,128,512]{2,1,0:T(8,128)(2,1)S(1)}, bf16[1,128,512]{2,1,0:T(8,128)(2,1)S(1)}, u32[]{:S(2)}, u32[]{:S(2)}) collective-permute-start(bf16[1,128,512]{2,1,0:T(8,128)(2,1)S(1)} %get-tuple-element.209), channel_id=1, source_target_pairs={{0,7},{1,0},{2,1},{3,2},{4,3},{5,4},{6,5},{7,6},{8,15},{9,8},{10,9... | collective-permute-start | bytes 393224 | tf_op jit(solution)/shard_map/ppermute | solution.py:16
  136.7 9.3 %collective-permute-start.15 = (bf16[1,128,512]{2,1,0:T(8,128)(2,1)S(1)}, bf16[1,128,512]{2,1,0:T(8,128)(2,1)S(1)}, u32[]{:S(2)}, u32[]{:S(2)}) collective-permute-start(bf16[1,128,512]{2,1,0:T(8,128)(2,1)S(1)} %get-tuple-element.208), channel_id=1, source_target_pairs={{0,6},{1,7},{2,0},{3,1},{4,2},{5,3},{6,4},{7,5},{8,14},{9,15},{10,... | collective-permute-start | bytes 393224 | tf_op jit(solution)/shard_map/ppermute | solution.py:16
  140.9 5.5 %collective-permute-start.16 = (bf16[1,128,512]{2,1,0:T(8,128)(2,1)S(1)}, bf16[1,128,512]{2,1,0:T(8,128)(2,1)S(1)}, u32[]{:S(2)}, u32[]{:S(2)}) collective-permute-start(bf16[1,128,512]{2,1,0:T(8,128)(2,1)S(1)} %get-tuple-element.207), channel_id=1, source_target_pairs={{0,5},{1,6},{2,7},{3,0},{4,1},{5,2},{6,3},{7,4},{8,13},{9,14},{10,... | collective-permute-start | bytes 393224 | tf_op jit(solution)/shard_map/ppermute | solution.py:16
  141.6 20.0 %collective-permute-start.17 = (bf16[1,128,512]{2,1,0:T(8,128)(2,1)S(1)}, bf16[1,128,512]{2,1,0:T(8,128)(2,1)S(1)}, u32[]{:S(2)}, u32[]{:S(2)}) collective-permute-start(bf16[1,128,512]{2,1,0:T(8,128)(2,1)S(1)} %get-tuple-element.206), channel_id=1, source_target_pairs={{0,4},{1,5},{2,6},{3,7},{4,0},{5,1},{6,2},{7,3},{8,12},{9,13},{10,... | collective-permute-start | bytes 393224 | tf_op jit(solution)/shard_map/ppermute | solution.py:16
  143.2 19.7 %collective-permute-start.18 = (bf16[1,128,512]{2,1,0:T(8,128)(2,1)S(1)}, bf16[1,128,512]{2,1,0:T(8,128)(2,1)S(1)}, u32[]{:S(2)}, u32[]{:S(2)}) collective-permute-start(bf16[1,128,512]{2,1,0:T(8,128)(2,1)S(1)} %get-tuple-element.205), channel_id=1, source_target_pairs={{0,3},{1,4},{2,5},{3,6},{4,7},{5,0},{6,1},{7,2},{8,11},{9,12},{10,... | collective-permute-start | bytes 393224 | tf_op jit(solution)/shard_map/ppermute | solution.py:16
  143.2 19.7 %collective-permute-start.19 = (bf16[1,128,512]{2,1,0:T(8,128)(2,1)S(1)}, bf16[1,128,512]{2,1,0:T(8,128)(2,1)S(1)}, u32[]{:S(2)}, u32[]{:S(2)}) collective-permute-start(bf16[1,128,512]{2,1,0:T(8,128)(2,1)S(1)} %get-tuple-element.204), channel_id=1, source_target_pairs={{0,2},{1,3},{2,4},{3,5},{4,6},{5,7},{6,0},{7,1},{8,10},{9,11},{10,... | collective-permute-start | bytes 393224 | tf_op jit(solution)/shard_map/ppermute | solution.py:16
  146.0 17.0 %collective-permute-start.20 = (bf16[1,128,512]{2,1,0:T(8,128)(2,1)S(1)}, bf16[1,128,512]{2,1,0:T(8,128)(2,1)S(1)}, u32[]{:S(2)}, u32[]{:S(2)}) collective-permute-start(bf16[1,128,512]{2,1,0:T(8,128)(2,1)S(1)} %get-tuple-element.203), channel_id=1, source_target_pairs={{0,1},{1,2},{2,3},{3,4},{4,5},{5,6},{6,7},{7,0},{8,9},{9,10},{10,1... | collective-permute-start | bytes 393224 | tf_op jit(solution)/shard_map/ppermute | solution.py:16
  171.2 0.8 copy-start.6
  172.0 2.3 copy-start.10
  179.5 6.8 %collective-permute-start.21 = (bf16[1,128,512]{2,1,0:T(8,128)(2,1)S(1)}, bf16[1,128,512]{2,1,0:T(8,128)(2,1)S(1)}, u32[]{:S(2)}, u32[]{:S(2)}) collective-permute-start(bf16[1,128,512]{2,1,0:T(8,128)(2,1)S(1)} %get-tuple-element.202), channel_id=1, source_target_pairs={{0,7},{1,0},{2,1},{3,2},{4,3},{5,4},{6,5},{7,6},{8,15},{9,8},{10,9... | collective-permute-start | bytes 393224 | tf_op jit(solution)/shard_map/ppermute | solution.py:16
  179.5 9.2 %collective-permute-start.22 = (bf16[1,128,512]{2,1,0:T(8,128)(2,1)S(1)}, bf16[1,128,512]{2,1,0:T(8,128)(2,1)S(1)}, u32[]{:S(2)}, u32[]{:S(2)}) collective-permute-start(bf16[1,128,512]{2,1,0:T(8,128)(2,1)S(1)} %get-tuple-element.201), channel_id=1, source_target_pairs={{0,6},{1,7},{2,0},{3,1},{4,2},{5,3},{6,4},{7,5},{8,14},{9,15},{10,... | collective-permute-start | bytes 393224 | tf_op jit(solution)/shard_map/ppermute | solution.py:16
  183.8 5.2 %collective-permute-start.23 = (bf16[1,128,512]{2,1,0:T(8,128)(2,1)S(1)}, bf16[1,128,512]{2,1,0:T(8,128)(2,1)S(1)}, u32[]{:S(2)}, u32[]{:S(2)}) collective-permute-start(bf16[1,128,512]{2,1,0:T(8,128)(2,1)S(1)} %get-tuple-element.200), channel_id=1, source_target_pairs={{0,5},{1,6},{2,7},{3,0},{4,1},{5,2},{6,3},{7,4},{8,13},{9,14},{10,... | collective-permute-start | bytes 393224 | tf_op jit(solution)/shard_map/ppermute | solution.py:16
  184.4 20.1 %collective-permute-start.24 = (bf16[1,128,512]{2,1,0:T(8,128)(2,1)S(1)}, bf16[1,128,512]{2,1,0:T(8,128)(2,1)S(1)}, u32[]{:S(2)}, u32[]{:S(2)}) collective-permute-start(bf16[1,128,512]{2,1,0:T(8,128)(2,1)S(1)} %get-tuple-element.199), channel_id=1, source_target_pairs={{0,4},{1,5},{2,6},{3,7},{4,0},{5,1},{6,2},{7,3},{8,12},{9,13},{10,... | collective-permute-start | bytes 393224 | tf_op jit(solution)/shard_map/ppermute | solution.py:16
  186.1 19.7 %collective-permute-start.25 = (bf16[1,128,512]{2,1,0:T(8,128)(2,1)S(1)}, bf16[1,128,512]{2,1,0:T(8,128)(2,1)S(1)}, u32[]{:S(2)}, u32[]{:S(2)}) collective-permute-start(bf16[1,128,512]{2,1,0:T(8,128)(2,1)S(1)} %get-tuple-element.198), channel_id=1, source_target_pairs={{0,3},{1,4},{2,5},{3,6},{4,7},{5,0},{6,1},{7,2},{8,11},{9,12},{10,... | collective-permute-start | bytes 393224 | tf_op jit(solution)/shard_map/ppermute | solution.py:16
  186.3 19.6 %collective-permute-start.26 = (bf16[1,128,512]{2,1,0:T(8,128)(2,1)S(1)}, bf16[1,128,512]{2,1,0:T(8,128)(2,1)S(1)}, u32[]{:S(2)}, u32[]{:S(2)}) collective-permute-start(bf16[1,128,512]{2,1,0:T(8,128)(2,1)S(1)} %get-tuple-element.197), channel_id=1, source_target_pairs={{0,2},{1,3},{2,4},{3,5},{4,6},{5,7},{6,0},{7,1},{8,10},{9,11},{10,... | collective-permute-start | bytes 393224 | tf_op jit(solution)/shard_map/ppermute | solution.py:16
  188.7 17.1 %collective-permute-start.27 = (bf16[1,128,512]{2,1,0:T(8,128)(2,1)S(1)}, bf16[1,128,512]{2,1,0:T(8,128)(2,1)S(1)}, u32[]{:S(2)}, u32[]{:S(2)}) collective-permute-start(bf16[1,128,512]{2,1,0:T(8,128)(2,1)S(1)} %get-tuple-element.196), channel_id=1, source_target_pairs={{0,1},{1,2},{2,3},{3,4},{4,5},{5,6},{6,7},{7,0},{8,9},{9,10},{10,1... | collective-permute-start | bytes 393224 | tf_op jit(solution)/shard_map/ppermute | solution.py:16
  207.3 10.0 %copy-start.3 = (f32[512,512]{1,0:T(8,128)S(1)}, f32[512,512]{1,0:T(8,128)}, u32[]{:S(2)}) copy-start(f32[512,512]{1,0:T(8,128)} %fusion.53) | copy-start | bytes 3145732
  217.3 2.0 copy-start.17
  217.3 2.0 copy-start.18
  219.0 1.0 copy-start.7
  219.0 1.2 copy-start.8
  219.0 1.3 copy-start.9
  247.6 2.3 copy-start.1
Sparse Core Ops, SparseCore 0:
  9.2 37.9 all-gather.4
  49.0 35.1 all-gather.6
